TPU v7x, 1024 devices: a whole 4x4x32 slice. The times are simulated.
1024 devices in a mesh: ctx: 16 (over x, z_hi), tp: 16 (over z_lo, core), grp: 4 (over y).
Axes of the slice: x: 4, y: 4, z: 32 (z_hi: 4, z_lo: 8; z = z_hi * 8 + z_lo), core: 2. Of those that a mesh axis runs over, the one named last changes fastest.
Arguments:
- pre_act: bfloat16 [16384, 5120], P(('ctx', 'grp')), may hold values from -6 to 6
- w_out: bfloat16 [5120, 8192], P(None, 'tp'), may hold values from -0.078125 to 0.078125
- b_out: bfloat16 [8192], P('tp'), may hold values from -3 to 3
- row_slot: int32 [16384], P(('ctx', 'grp')), may hold values from 0 to 511, as said below
- ctx_slot: int32 [32768], P(('ctx', 'grp')), may hold values from -1 to 511, as said below
- text_rows: bfloat16 [32768, 8192], P(('ctx', 'grp'), 'tp'), may hold values from -6 to 6
- cotangent: bfloat16 [32768, 8192], P(('ctx', 'grp'), 'tp'), may hold values from -6 to 6
Outputs:
- embeds: bfloat16 [32768, 8192], P(('ctx', 'grp'), 'tp')
- grad_pre: bfloat16 [16384, 5120], P(('ctx', 'grp'))
Inputs may be any that keep to these rules, and one draw needn't show every extreme that they name: `row_slot`: within each aligned block of 256 rows (one encoder device) the values are distinct; value // 8 is the context shard (index along ctx+grp) that receives the row and value % 8 its slot there; in every block some shard receives exactly 8 rows. `ctx_slot`: within each aligned block of 512 positions (one context shard) the values other than -1 are distinct; a value s names the row that encoder device s // 8 (index along ctx+grp) sent in slot s % 8 to this shard; every image token is placed at exactly one position and every used slot names a sent row.
All inputs are finite; a program needn't handle non-finite values.
Results may differ from a plain program's by a relative error of at most 0.018.
Values may be sent and summed in bfloat16 or wider, within the bound.
A program may use at most 64 MiB of HBM per device.

v0:
```python
import jax
import jax.numpy as jnp
from jax import lax
from jax.sharding import Mesh
from jax.sharding import PartitionSpec as P

TP = ("tp_0", "tp_1")


def split_up(array, dim, peers):
    lengths = array.shape
    pieces = array.reshape(*lengths[:dim], peers, lengths[dim] // peers, *lengths[dim + 1 :])
    return jnp.moveaxis(pieces, dim, 0)


def joined_along(pieces, dim):
    pieces = jnp.moveaxis(pieces, 0, dim)
    lengths = pieces.shape
    return pieces.reshape(*lengths[:dim], lengths[dim] * lengths[dim + 1], *lengths[dim + 2 :])


def exchange_both(array, axis, axes, splits, concats):
    sizes = [lax.axis_size(a) for a in axes]
    pieces = split_up(array, splits[0], sizes[0])
    pieces = jnp.moveaxis(split_up(pieces, splits[1] + 1, sizes[1]), 0, 1)
    inside = pieces.shape[2:]
    pieces = pieces.reshape(-1, *inside)
    pieces = lax.all_to_all(pieces, axis, split_axis=0, concat_axis=0, tiled=True)
    pieces = joined_along(pieces.reshape(*sizes, *inside), concats[0] + 1)
    return joined_along(pieces, concats[1])


def padded_to(lines, peers):
    spare = -len(lines) % peers
    return jnp.pad(lines, [(0, spare)] + [(0, 0)] * (lines.ndim - 1))


def sum_by_parts(array, near, far):
    lines = array.reshape(-1, *array.shape[1:][-1:])
    padded = padded_to(lines, lax.axis_size(near))
    own = lax.psum_scatter(padded, near, scatter_dimension=0, tiled=True)
    own = lax.psum(own, far)
    whole = lax.all_gather(own, near, axis=0, tiled=True)
    return whole[: len(lines)].reshape(array.shape)


def gelu_value(values):
    return 0.5 * values * (1.0 + lax.erf(values * 0.7071067811865476))


def gelu_slope(values):
    return (
        0.5 * (1.0 + lax.erf(values * 0.7071067811865476))
        + values * jnp.exp(-0.5 * values * values) * 0.3989422804014327
    )


def shards(pre_act, w_out, b_out, row_slot, ctx_slot, text_rows, cotangent):
    ctx_count = lax.axis_size("ctx")
    grp_count = lax.axis_size("grp")
    groups = ctx_count * grp_count
    row_count = pre_act.shape[0]
    slot_count = 2 * row_count
    capacity = slot_count // groups
    width = w_out.shape[1]
    pre_float = pre_act.astype(jnp.float32)
    hidden = gelu_value(pre_float).astype(jnp.bfloat16)
    merged = (
        jnp.dot(hidden, w_out, preferred_element_type=jnp.float32) + b_out.astype(jnp.float32)
    ).astype(jnp.bfloat16)
    outgoing = jnp.zeros((slot_count, width), jnp.bfloat16).at[row_slot].set(merged)
    placed = ctx_slot >= 0
    returning = (
        jnp.zeros((slot_count, width), jnp.bfloat16)
        .at[jnp.where(placed, ctx_slot, slot_count)]
        .set(cotangent, mode="drop")
    )
    arrived = exchange_both(
        outgoing.reshape(ctx_count, grp_count, capacity, width),
        ("ctx", "grp"),
        ("ctx", "grp"),
        (0, 1),
        (0, 1),
    )
    returned = exchange_both(
        returning.reshape(ctx_count, grp_count, capacity, width),
        ("ctx", "grp"),
        ("ctx", "grp"),
        (0, 1),
        (0, 1),
    )
    arrived = arrived.reshape(slot_count, width)
    embeds = jnp.where(placed[:, None], arrived[jnp.where(placed, ctx_slot, 0)], text_rows)
    grad_rows = returned.reshape(slot_count, width)[row_slot]
    partial_value = lax.dot_general(
        grad_rows, w_out, (((1,), (1,)), ((), ())), preferred_element_type=jnp.float32
    )
    term = partial_value.astype(jnp.bfloat16)
    summed = sum_by_parts(term, "tp_1", "tp_0").astype(jnp.float32)
    grad_pre = (summed * gelu_slope(pre_float)).astype(jnp.bfloat16)
    return (embeds, grad_pre)


def solution(mesh):
    split = Mesh(
        mesh.devices.reshape(mesh.shape["ctx"], 8, 2, mesh.shape["grp"]),
        ("ctx", "tp_0", "tp_1", "grp"),
    )
    in_specs = (
        P(("ctx", "grp"), None),
        P(None, TP),
        P(TP),
        P(("ctx", "grp")),
        P(("ctx", "grp")),
        P(("ctx", "grp"), TP),
        P(("ctx", "grp"), TP),
    )
    out_specs = (P(("ctx", "grp"), TP), P(("ctx", "grp"), None))
    return jax.shard_map(
        shards, mesh=split, in_specs=in_specs, out_specs=out_specs, check_vma=False
    )
```

profile of v0, /device:TPU:1, one launch (start us, length us, event | category | flops | bytes accessed | tf_op | source)
XLA Modules:
  0.0 334.5 jit_solution(12029386151437779749)
XLA Ops:
  7.2 0.7 compare_select_fusion
  7.9 3.7 %scatter_custom_fusion.1 = bf16[512,512]{1,0:T(8,128)(2,1)} fusion(s32[512]{0:T(512)S(1)} %get-tuple-element.2, bf16[512,512]{1,0:T(8,128)(2,1)} %param.13, bf16[]{:T(256)} %constant.9.clone.1), kind=kCustom, calls=%fused_computation.24 | custom fusion | bytes 524800 | tf_op jit(solution)/shard_map/scatter | solution.py:76
  11.5 35.0 %all-to-all-start.1 = ((bf16[64,1,1,8,512]{4,3,2,1,0:T(8,128)(2,1)}), bf16[64,1,1,8,512]{4,3,2,1,0:T(8,128)(2,1)S(1)}, u32[]{:S(2)}, u32[]{:S(2)}) async-start(bf16[64,1,1,8,512]{4,3,2,1,0:T(8,128)(2,1)} %bitcast.8), calls=%async_computation.1 | async-start | bytes 1048576 | tf_op jit(solution)/shard_map/all_to_all | solution.py:28
  46.5 0.0 reduce-scatter.2.cloned.1.call-start
  46.5 0.7 compare_select_fusion.2
  47.2 51.3 %all-to-all-done.1 = bf16[64,1,1,8,512]{4,3,2,1,0:T(8,128)(2,1)S(1)} async-done(((bf16[64,1,1,8,512]{4,3,2,1,0:T(8,128)(2,1)}), bf16[64,1,1,8,512]{4,3,2,1,0:T(8,128)(2,1)S(1)}, u32[]{:S(2)}, u32[]{:S(2)}) %all-to-all-start.1) | async-done | bytes 524320 | tf_op jit(solution)/shard_map/all_to_all | solution.py:28
  98.5 1.2 gather_fusion.1
  99.7 0.0 copy-start.2
  99.7 0.0 copy-start
  99.7 5.7 %convolution_convert_fusion = bf16[256,5120]{1,0:T(8,128)(2,1)} fusion(bf16[256,512]{1,0:T(8,128)(2,1)S(1)} %gather_fusion.1, bf16[5120,512]{1,0:T(8,128)(2,1)} %param.8), kind=kOutput, calls=%fused_computation.9 | convolution fusion | flops 1343488000 | bytes 8126464 | tf_op jit(solution)/shard_map/dot_general | solution.py:95
  105.4 0.0 reduce-scatter.2.cloned.1.call-update
  105.4 0.0 copy-done.2
  105.5 0.0 copy-done
  105.5 0.0 copy-start.1
  105.5 4.0 %fusion.15 = bf16[256,512]{1,0:T(8,128)(2,1)S(1)} fusion(bf16[5120,512]{1,0:T(8,128)(2,1)} %param.8, bf16[256,5120]{1,0:T(8,128)(2,1)S(1)} %copy-done, f32[512]{0:T(512)S(1)} %convert_element_type.23), kind=kOutput, calls=%fused_computation.22 | convolution fusion | flops 1350303744 | bytes 8128512 | tf_op jit(solution)/shard_map/dot_general | solution.py:69
  109.5 2.3 scatter_custom_fusion
  111.8 16.3 %all-to-all-start = ((bf16[64,1,1,8,512]{4,3,2,1,0:T(8,128)(2,1)}), bf16[64,1,1,8,512]{4,3,2,1,0:T(8,128)(2,1)S(1)}, u32[]{:S(2)}, u32[]{:S(2)}) async-start(bf16[64,1,1,8,512]{4,3,2,1,0:T(8,128)(2,1)} %bitcast.29), calls=%async_computation | async-start | bytes 1048576 | tf_op jit(solution)/shard_map/all_to_all | solution.py:28
  128.1 0.0 all-reduce.2.cloned.1.call-start
  128.2 7.0 %reduce-scatter.2.cloned.1.call-done = bf16[128,5120]{1,0:T(8,128)(2,1)} async-done(((bf16[256,5120]{1,0:T(8,128)(2,1)}), bf16[128,5120]{1,0:T(8,128)(2,1)}) %reduce-scatter.2.cloned.1.call-update) | async-done | bytes 1310736 | tf_op jit(solution)/shard_map/reduce_scatter | solution.py:41
  135.2 0.0 all-reduce.2.cloned.1.call-update
  135.2 0.0 all-gather.2.cloned.1.call-start
  135.3 149.9 %all-reduce.2.cloned.1.call-done = bf16[128,5120]{1,0:T(8,128)(2,1)} async-done(((bf16[128,5120]{1,0:T(8,128)(2,1)}), bf16[128,5120]{1,0:T(8,128)(2,1)}) %all-reduce.2.cloned.1.call-update) | async-done | bytes 1310736 | tf_op jit(solution)/shard_map/psum | solution.py:42
  285.1 0.0 all-gather.2.cloned.1.call-update
  285.2 0.0 copy-done.1
  285.2 0.0 all-to-all-done
  285.2 2.6 gather_fusion
  287.8 2.1 broadcast_select_fusion
  290.0 32.7 %all-gather.2.cloned.1.call-done = bf16[256,5120]{1,0:T(8,128)(2,1)} async-done(((bf16[128,5120]{1,0:T(8,128)(2,1)}), bf16[256,5120]{1,0:T(8,128)(2,1)}) %all-gather.2.cloned.1.call-update) | async-done | bytes 2621456 | tf_op jit(solution)/shard_map/all_gather | solution.py:43
  322.7 5.2 %fusion.8 = bf16[256,5120]{1,0:T(8,128)(2,1)} fusion(bf16[256,5120]{1,0:T(8,128)(2,1)S(1)} %copy-done, bf16[256,5120]{1,0:T(8,128)(2,1)} %all-gather.2.cloned.1.call-done), kind=kLoop, calls=%fused_computation.18 | loop fusion | flops 15728640 | bytes 7864320 | tf_op jit(solution)/shard_map/convert_element_type | solution.py:100
  (4 shorter events, 0.0 us)
Async XLA Ops:
  11.5 87.0 %all-to-all-start.1 = ((bf16[64,1,1,8,512]{4,3,2,1,0:T(8,128)(2,1)}), bf16[64,1,1,8,512]{4,3,2,1,0:T(8,128)(2,1)S(1)}, u32[]{:S(2)}, u32[]{:S(2)}) async-start(bf16[64,1,1,8,512]{4,3,2,1,0:T(8,128)(2,1)} %bitcast.8), calls=%async_computation.1 | async-start | bytes 1048576 | tf_op jit(solution)/shard_map/all_to_all | solution.py:28
  46.5 88.7 %reduce-scatter.2.cloned.1.call-start = ((), (), s32[]{:S(2)}) async-start(), calls=%async_computation.3 | async-start | bytes 3932160 | tf_op jit(solution)/shard_map/reduce_scatter | solution.py:41
  99.7 5.7 %copy-start.2 = (bf16[512]{0:T(512)(128)(2,1)S(1)}, bf16[512]{0:T(512)(128)(2,1)}, u32[]{:S(2)}) copy-start(bf16[512]{0:T(512)(128)(2,1)} %param.9) | copy-start | bytes 3076
  99.7 5.8 %copy-start = (bf16[256,5120]{1,0:T(8,128)(2,1)S(1)}, bf16[256,5120]{1,0:T(8,128)(2,1)}, u32[]{:S(2)}) copy-start(bf16[256,5120]{1,0:T(8,128)(2,1)} %param.7) | copy-start | bytes 7864324
  105.5 179.7 %copy-start.1 = (s32[512]{0:T(512)S(1)}, s32[512]{0:T(512)}, u32[]{:S(2)}) copy-start(s32[512]{0:T(512)} %param.11) | copy-start | bytes 6148
  111.8 173.4 %all-to-all-start = ((bf16[64,1,1,8,512]{4,3,2,1,0:T(8,128)(2,1)}), bf16[64,1,1,8,512]{4,3,2,1,0:T(8,128)(2,1)S(1)}, u32[]{:S(2)}, u32[]{:S(2)}) async-start(bf16[64,1,1,8,512]{4,3,2,1,0:T(8,128)(2,1)} %bitcast.29), calls=%async_computation | async-start | bytes 1048576 | tf_op jit(solution)/shard_map/all_to_all | solution.py:28
  128.1 157.0 %all-reduce.2.cloned.1.call-start = ((), (), s32[]{:S(2)}) async-start(), calls=%async_computation.4 | async-start | bytes 2621440 | tf_op jit(solution)/shard_map/psum | solution.py:42
  135.2 187.5 %all-gather.2.cloned.1.call-start = ((), (), s32[]{:S(2)}) async-start(), calls=%async_computation.5 | async-start | bytes 3932160 | tf_op jit(solution)/shard_map/all_gather | solution.py:43
Sparse Core Ops, SparseCore 0:
  105.6 29.5 reduce-scatter.1
  138.7 146.3 all-reduce.1
  287.8 34.8 all-gather.1
where the time goes:
time: 335 us; the launch traced here: 334 us
  waiting for transfers between devices  241 us (72%)
  starting transfers between devices  51.4 us (15%)
  between operations  13.8 us (4%)
  local copies, waits for them, and re-layouts  9.77 us (3%)
  matrix products  9.71 us (3%)
  other arithmetic  8.77 us (3%)
    psum x1, waiting for transfers between devices, sum_by_parts(): own = lax.psum(own, far)  150 us
    all_to_all x2, waiting for transfers between devices, exchange_both(): lax.all_to_all(pieces, axis, split_axis=0, concat_axis=0, tiled=True)  51.3 us
    all_to_all x2, starting transfers between devices, exchange_both(): lax.all_to_all(pieces, axis, split_axis=0, concat_axis=0, tiled=True)  51.3 us
    all_gather x1, waiting for transfers between devices, sum_by_parts(): whole = lax.all_gather(own, near, axis=0, tiled=True)  32.7 us
    reduce_scatter x1, waiting for transfers between devices, sum_by_parts(): own = lax.psum_scatter(padded, near, scatter_dimension=0, tiled=True)  7 us
  transfers between devices with their start and end apart: 5, of which 4 were waited for; matrix products, arithmetic and copies ran while one was open for 4% of the time, Pallas kernels for 0%

commit v1 on v0

v1 whole, which is shorter than its diff:
```python
import functools

import jax
import jax.numpy as jnp
from jax import lax
from jax.experimental import pallas as pl
from jax.experimental.pallas import tpu as pltpu
from jax.sharding import Mesh
from jax.sharding import PartitionSpec as P

MESH = pl.DeviceIdType.MESH
CHUNKS = 20
LAG = 3


def gelu_value(values):
    return 0.5 * values * (1.0 + lax.erf(values * 0.7071067811865476))


def gelu_slope(values):
    return (
        0.5 * (1.0 + lax.erf(values * 0.7071067811865476))
        + values * jnp.exp(-0.5 * values * values) * 0.3989422804014327
    )


def remote(src, dst, send, recv, peer):
    return pltpu.make_async_remote_copy(
        src_ref=src, dst_ref=dst, send_sem=send, recv_sem=recv, device_id=peer, device_id_type=MESH
    )


def nt_dot(left, right):
    return lax.dot_general(
        left, right, (((1,), (1,)), ((), ())), preferred_element_type=jnp.float32
    )


def kernel(
    sizes, cap,
    merged, cot, text, w, pre, row_out, tok_out, row_in, tok_in,
    emb, grad,
    out_buf, z_buf, relay, x_buf, y_buf, w_far, rows_full, rows_far, flow_in, flow_out, acc,
    z_send, z_recv, x_send, x_recv, y_send, y_recv,
    w_send, w_recv, g_send, g_recv,
    flow_send, flow_recv, fin_send, fin_recv, mate_send, mate_recv,
):
    nz, nx, ny, nl = sizes
    zh, xx, yy = lax.axis_index("zh"), lax.axis_index("x"), lax.axis_index("y")
    line, core = lax.axis_index("zl"), lax.axis_index("core")
    mate = {"core": 1 - core}
    right, left = {"zh": lax.rem(zh + 1, nz)}, {"zh": lax.rem(zh + nz - 1, nz)}
    up, down = {"zl": line + 1}, {"zl": line - 1}
    x_peer = [{"x": lax.rem(xx + e, nx)} for e in range(nx)]
    y_peer = [{"y": lax.rem(yy + f, ny)} for f in range(ny)]
    blocks = nz * nx * ny
    slots = blocks * 2 * cap
    tokens, width = cot.shape
    half_width = width // 2
    rows = merged.shape[0]
    half_rows = rows // 2
    count, piece = flow_out.shape[0], flow_out.shape[2]
    shape6 = (nz, nx, ny, 2 * cap, half_width)

    middle = nl // 2 - 1 + core if nl > 1 else 0 * core
    has_low = jnp.logical_and(line <= middle, line > 0)
    has_high = jnp.logical_and(line >= middle, line < nl - 1)

    barrier = pltpu.get_barrier_semaphore()
    greeted = [mate] + x_peer[1:] + y_peer[1:]
    if nz > 1:
        greeted += [right, left]
    for peer in greeted:
        pl.semaphore_signal(barrier, inc=1, device_id=peer, device_id_type=MESH)

    @pl.when(line > 0)
    def _():
        pl.semaphore_signal(barrier, inc=1, device_id=down, device_id_type=MESH)

    @pl.when(line < nl - 1)
    def _():
        pl.semaphore_signal(barrier, inc=1, device_id=up, device_id_type=MESH)

    pl.semaphore_wait(
        barrier,
        len(greeted) + (line > 0).astype(jnp.int32) + (line < nl - 1).astype(jnp.int32),
    )

    def place(b, source, where):
        total = jnp.zeros((slots, half_width), jnp.float32)
        ids = lax.broadcasted_iota(jnp.int32, (slots, source.shape[0]), 0)
        for h in range(2):
            hot = (ids == where[...] + h * cap).astype(jnp.bfloat16)
            part = source[:, h * half_width : (h + 1) * half_width]
            total += jnp.dot(hot, part, preferred_element_type=jnp.float32)
        out_buf[b] = total.astype(jnp.bfloat16).reshape(shape6)

    def pick(b, where, h):
        ids = lax.broadcasted_iota(jnp.int32, (where.shape[0], slots), 1)
        hot = (ids == where[...] + h * cap).astype(jnp.bfloat16)
        data = y_buf[b].reshape(slots, half_width)
        return jnp.dot(hot, data, preferred_element_type=jnp.float32)

    cut = nx // 2

    def z_copy(b, n):
        src, dst, peer = (
            lambda: (out_buf.at[b, 2, :cut], relay.at[b, 0], right),
            lambda: (out_buf.at[b, 2, cut:], relay.at[b, 1], left),
            lambda: (out_buf.at[b, 1], z_buf.at[b, 0], right),
            lambda: (out_buf.at[b, 3], z_buf.at[b, 2], left),
            lambda: (relay.at[b, 0], z_buf.at[b, 1, :cut], right),
            lambda: (relay.at[b, 1], z_buf.at[b, 1, cut:], left),
        )[n]()
        return remote(src, dst, z_send.at[b, n], z_recv.at[b, n], peer)

    def x_copy(b, d, e):
        src = out_buf.at[b, 0, e] if d == 0 else z_buf.at[b, d - 1, e]
        dst = x_buf.at[b, d, e]
        if e == 0:
            return pltpu.make_async_copy(src, dst, x_recv.at[b, d, 0])
        return remote(src, dst, x_send.at[b, d, e], x_recv.at[b, d, e], x_peer[e])

    def y_copy(b, d, f):
        src, dst = x_buf.at[b, d, :, f], y_buf.at[b, d, :, f]
        if f == 0:
            return pltpu.make_async_copy(src, dst, y_recv.at[b, d, 0])
        return remote(src, dst, y_send.at[b, d, f], y_recv.at[b, d, f], y_peer[f])

    def z_start(b):
        if nz > 1:
            for n in range(4):
                z_copy(b, n).start()

    def z_forward(b):
        if nz > 1:
            for n in (0, 1):
                z_copy(b, n).wait_recv()
                z_copy(b, n + 4).start()

    def z_arrive(b, d):
        for n in {0: (), 1: (2,), 2: (4, 5), 3: (3,)}[d]:
            z_copy(b, n).wait_recv()

    def x_start(b, d):
        for e in list(range(1, nx)) + [0]:
            x_copy(b, d, e).start()

    def y_start(b, d):
        x_copy(b, d, 0).wait()
        for e in range(1, nx):
            x_copy(b, d, e).wait_recv()
        for f in list(range(1, ny)) + [0]:
            y_copy(b, d, f).start()

    def y_arrive(b, d):
        y_copy(b, d, 0).wait()
        for f in range(1, ny):
            y_copy(b, d, f).wait_recv()

    w_copy = remote(w, w_far, w_send, w_recv, mate)
    w_copy.start()

    place(0, cot, tok_out)
    z_start(0)
    x_start(0, 0)
    place(1, merged, row_out)
    y_start(0, 0)
    z_forward(0)
    z_start(1)
    x_start(1, 0)
    y_start(1, 0)
    far = [1, 3, 2] if nz > 1 else []
    for d in far:
        z_arrive(0, d)
        x_start(0, d)
        y_start(0, d)
    for d in range(nz):
        y_arrive(0, d)

    for h in range(2):
        rows_full[:, h * half_width : (h + 1) * half_width] = pick(0, row_in, h).astype(
            jnp.bfloat16
        )
    mine = pl.ds(pl.multiple_of(core * half_rows, half_rows), half_rows)
    other = pl.ds(pl.multiple_of((1 - core) * half_rows, half_rows), half_rows)
    g_copy = remote(rows_full.at[other], rows_far, g_send, g_recv, mate)
    g_copy.start()
    z_forward(1)
    w_copy.wait_recv()
    g_copy.wait_recv()

    def columns(i):
        return pl.ds(pl.multiple_of(i * piece, piece), piece)

    def flow_copy(i, side, peer):
        return remote(
            flow_out.at[i], flow_in.at[side, i], flow_send.at[i], flow_recv.at[side, i], peer
        )

    def fin_copy(i, side, peer):
        block = grad.at[mine, columns(i)]
        return remote(block, block, fin_send.at[side, i], fin_recv.at[i], peer)

    def mate_copy(i):
        block = grad.at[mine, columns(i)]
        return remote(block, block, mate_send.at[i], mate_recv.at[i], mate)

    def mate_block(i):
        block = grad.at[other, columns(i)]
        return remote(block, block, mate_send.at[i], mate_recv.at[i], mate)

    def publish(i):
        @pl.when(has_low)
        def _():
            fin_copy(i, 0, down).start()

        @pl.when(has_high)
        def _():
            fin_copy(i, 1, up).start()

        mate_copy(i).start()

    away = jnp.where(line < middle, middle - line, line - middle)
    lag = 1 + LAG * away
    steps = count + 1 + LAG * (nl // 2 + (1 if nl > 1 else 0))

    def step(i, carry):
        @pl.when(i < count)
        def _():
            acc[...] = nt_dot(rows_full[mine, :], w[columns(i), :]) + nt_dot(
                rows_far[...], w_far[columns(i), :]
            )

            @pl.when(has_low)
            def _():
                flow_copy(i, 0, up).wait_recv()
                acc[...] += flow_in[0, i].astype(jnp.float32)

            @pl.when(has_high)
            def _():
                flow_copy(i, 1, down).wait_recv()
                acc[...] += flow_in[1, i].astype(jnp.float32)

            @pl.when(line != middle)
            def _():
                flow_out[i] = acc[...].astype(jnp.bfloat16)

            @pl.when(line < middle)
            def _():
                flow_copy(i, 0, up).start()

            @pl.when(line > middle)
            def _():
                flow_copy(i, 1, down).start()

            @pl.when(line == middle)
            def _():
                slope = gelu_slope(pre[mine, columns(i)].astype(jnp.float32))
                grad[mine, columns(i)] = (acc[...] * slope).astype(jnp.bfloat16)
                publish(i)

        j = i - lag

        @pl.when(jnp.logical_and(line != middle, jnp.logical_and(j >= 0, j < count)))
        def _():
            fin_copy(j, 0, down).wait_recv()
            publish(j)

        return carry

    first, second = count // 2, count // 2 + 3
    lax.fori_loop(0, first, step, 0)
    for d in far:
        z_arrive(1, d)
        x_start(1, d)
    lax.fori_loop(first, second, step, 0)
    for d in far:
        y_start(1, d)
    lax.fori_loop(second, steps, step, 0)

    for d in range(nz):
        y_arrive(1, d)
    for h in range(2):
        part = pl.ds(h * half_width, half_width)
        emb[:, part] = jnp.where(
            tok_in[...] >= 0, pick(1, tok_in, h).astype(jnp.bfloat16), text[:, part]
        )

    def drain(i, carry):
        @pl.when(line < middle)
        def _():
            flow_copy(i, 0, up).wait_send()

        @pl.when(line > middle)
        def _():
            flow_copy(i, 1, down).wait_send()

        @pl.when(has_low)
        def _():
            fin_copy(i, 0, down).wait_send()

        @pl.when(has_high)
        def _():
            fin_copy(i, 1, up).wait_send()

        mate_copy(i).wait_send()
        mate_block(i).wait_recv()
        return carry

    lax.fori_loop(0, count, drain, 0)
    w_copy.wait_send()
    g_copy.wait_send()
    for b in range(2):
        if nz > 1:
            for n in range(6):
                z_copy(b, n).wait_send()
        for d in range(nz):
            for e in range(1, nx):
                x_copy(b, d, e).wait_send()
            for f in range(1, ny):
                y_copy(b, d, f).wait_send()


def shards(cap, pre_act, w_out, b_out, row_slot, ctx_slot, text_rows, cotangent):
    nx, nz, ny, nl = (lax.axis_size(a) for a in ("x", "zh", "y", "zl"))
    xx, zh, yy = (lax.axis_index(a) for a in ("x", "zh", "y"))
    rows, depth = pre_act.shape
    tokens, width = cotangent.shape
    hidden = gelu_value(pre_act.astype(jnp.float32)).astype(jnp.bfloat16)
    merged = (
        jnp.dot(hidden, w_out, preferred_element_type=jnp.float32) + b_out.astype(jnp.float32)
    ).astype(jnp.bfloat16)

    def position(values, sign):
        peer, slot = values // cap, values % cap
        dx = (sign * (peer // (nz * ny) - xx)) % nx
        dz = (sign * ((peer // ny) % nz - zh)) % nz
        dy = (sign * (peer % ny - yy)) % ny
        base = ((dz * nx + dx) * ny + dy) * 2 * cap + slot
        return jnp.where(values >= 0, base, -1000000)

    row_out = position(row_slot, 1).reshape(1, rows)
    tok_out = position(ctx_slot, 1).reshape(1, tokens)
    row_in = position(row_slot, -1).reshape(rows, 1)
    tok_in = position(ctx_slot, -1).reshape(tokens, 1)

    half_width, half_rows = width // 2, rows // 2
    piece = depth // CHUNKS
    block = (nx, ny, 2 * cap, half_width)
    dma = pltpu.SemaphoreType.DMA
    bf16 = jnp.bfloat16
    scratch = [
        pltpu.VMEM((2, nz, *block), bf16),
        pltpu.VMEM((2, max(nz - 1, 1), *block), bf16),
        pltpu.VMEM((2, 2, max(nx // 2, 1), *block[1:]), bf16),
        pltpu.VMEM((2, nz, *block), bf16),
        pltpu.VMEM((2, nz, *block), bf16),
        pltpu.VMEM((depth, width), bf16),
        pltpu.VMEM((rows, width), bf16),
        pltpu.VMEM((half_rows, width), bf16),
        pltpu.VMEM((2, CHUNKS, half_rows, piece), bf16),
        pltpu.VMEM((CHUNKS, half_rows, piece), bf16),
        pltpu.VMEM((half_rows, piece), jnp.float32),
        dma((2, 6)), dma((2, 6)),
        dma((2, nz, nx)), dma((2, nz, nx)),
        dma((2, nz, ny)), dma((2, nz, ny)),
        dma, dma, dma, dma,
        dma((CHUNKS,)), dma((2, CHUNKS)),
        dma((2, CHUNKS)), dma((CHUNKS,)),
        dma((CHUNKS,)), dma((CHUNKS,)),
    ]
    return pl.pallas_call(
        functools.partial(kernel, (nz, nx, ny, nl), cap),
        out_shape=(
            jax.ShapeDtypeStruct((tokens, width), bf16),
            jax.ShapeDtypeStruct((rows, depth), bf16),
        ),
        in_specs=[pl.BlockSpec(memory_space=pltpu.VMEM)] * 9,
        out_specs=(pl.BlockSpec(memory_space=pltpu.VMEM),) * 2,
        scratch_shapes=scratch,
        compiler_params=pltpu.CompilerParams(
            collective_id=0, has_side_effects=True, vmem_limit_bytes=60 << 20
        ),
    )(merged, cotangent, text_rows, w_out, pre_act, row_out, tok_out, row_in, tok_in)


def build(mesh, nx, nz, nl, cap):
    split = Mesh(
        mesh.devices.reshape(nx, nz, nl, 2, mesh.shape["grp"]), ("x", "zh", "zl", "core", "y")
    )
    ctx, tp = ("x", "zh", "y"), ("zl", "core")
    return jax.shard_map(
        functools.partial(shards, cap),
        mesh=split,
        in_specs=(P(ctx, None), P(None, tp), P(tp), P(ctx), P(ctx), P(ctx, tp), P(ctx, tp)),
        out_specs=(P(ctx, tp), P(ctx, None)),
        check_vma=False,
    )


def solution(mesh):
    return build(mesh, 4, mesh.shape["ctx"] // 4, mesh.shape["tp"] // 2, 8)
```

time: 335 us -> 207 us (0.62)
  waiting for transfers between devices: 241 us -> 0 us
  Pallas kernels: 0 us -> 188 us
  starting transfers between devices: 51.4 us -> 0 us
  between operations: 13.8 us -> 0.65 us
  matrix products: 9.71 us -> 5.52 us
  other arithmetic: 8.77 us -> 4.68 us
    pallas_call x0 -> x1, Pallas kernels: none -> 188 us  [shards(): pl.pallas_call(functools.partial(kernel, (nz, nx, ny, nl), cap), out_shap...]
    psum x1 -> x0, waiting for transfers between devices: 150 us -> none  [sum_by_parts(): own = lax.psum(own, far)]
    all_to_all x2 -> x0, waiting for transfers between devices: 51.3 us -> none  [exchange_both(): lax.all_to_all(pieces, axis, split_axis=0, concat_axis=0, tiled=True)]
    all_to_all x2 -> x0, starting transfers between devices: 51.3 us -> none  [exchange_both(): lax.all_to_all(pieces, axis, split_axis=0, concat_axis=0, tiled=True)]
    all_gather x1 -> x0, waiting for transfers between devices: 32.7 us -> none  [sum_by_parts(): whole = lax.all_gather(own, near, axis=0, tiled=True)]
    reduce_scatter x1 -> x0, waiting for transfers between devices: 7 us -> none  [sum_by_parts(): own = lax.psum_scatter(padded, near, scatter_dimension=0, tiled=True)]
    scatter x2 -> x0, local copies, waits for them, and re-layouts: 5.97 us -> none  [the longest x1 3.66 us: shards(): returning = jnp.zeros((slot_count, width), jnp.bfloat16).at[jnp.where(pla...]
    dot_general x1 -> x0, matrix products: 5.69 us -> none  [shards(): lax.dot_general(grad_rows, w_out, (((1,), (1,)), ((), ())), preferred_ele...]
  transfers between devices with their start and end apart: 5 -> 0, of which waited for: 4 -> 0; matrix products, arithmetic and copies ran while one was open for 4% -> 0% of each run, Pallas kernels for 0% -> 0%
where the time goes in v1:
time: 207 us; the launch traced here: 206 us
  Pallas kernels  188 us (91%)
  local copies, waits for them, and re-layouts  6.92 us (3%)
  matrix products  5.52 us (3%)
  other arithmetic  4.68 us (2%)
    pallas_call x1, Pallas kernels, shards(): pl.pallas_call(functools.partial(kernel, (nz, nx, ny, nl), cap), out_shap...  188 us
    dot_general x1, matrix products, shards(): jnp.dot(hidden, w_out, preferred_element_type=jnp.float32)  5.52 us
    unnamed x2, local copies, waits for them, and re-layouts  5.27 us

profile of v1, /device:TPU:1, one launch (start us, length us, event | category | flops | bytes accessed | tf_op | source)
XLA Modules:
  0.0 206.2 jit_solution(11086690255589760608)
XLA Ops:
  0.6 0.7 convert_element_type.14
  1.3 0.7 add_select_fusion.12
  2.0 1.3 add_select_fusion.13
  3.3 0.7 fusion.34
  4.0 1.3 fusion.21
  5.3 0.8 copy.9.row_in
  6.1 0.9 copy.10.tok_in
  7.0 5.5 %fusion.9.merged = bf16[256,512]{1,0:T(8,128)(2,1)} fusion(bf16[5120,512]{1,0:T(8,128)(2,1)} %w.1, bf16[256,5120]{1,0:T(8,128)(2,1)} %pre.1, f32[512]{0:T(512)S(1)} %convert_element_type.14), kind=kOutput, calls=%fused_computation.8 | convolution fusion | flops 1350303744 | bytes 8128512 | tf_op jit(solution)/shard_map/dot_general | solution.py:332
  12.5 188.4 %shard_map.86 = (bf16[512,512]{1,0:T(8,128)(2,1)}, bf16[256,5120]{1,0:T(8,128)(2,1)}) custom-call(bf16[256,512]{1,0:T(8,128)(2,1)} %fusion.9.merged, bf16[512,512]{1,0:T(8,128)(2,1)} %cot.1, bf16[512,512]{1,0:T(8,128)(2,1)} %text.1, bf16[5120,512]{1,0:T(8,128)(2,1)} %w.1, bf16[256,5120]{1,0:T(8,128)(2,1)} %pre.1, s32[1,256]{1,0:T(1,128)} %bitcast.7, ...), custom_call_target="tpu_custom_call" | custom-call | tf_op jit(solution)/shard_map/pallas_call | solution.py:373
  200.9 1.9 copy.13
  202.8 3.4 %copy.14 = bf16[256,5120]{1,0:T(8,128)(2,1)} copy(bf16[256,5120]{1,0:T(8,128)(2,1)} %get-tuple-element.10) | data formatting | bytes 5242880

commit v2 on v1

--- a/solution.py
+++ b/solution.py
@@ -9,8 +9,8 @@
 from jax.sharding import PartitionSpec as P
 
 MESH = pl.DeviceIdType.MESH
-CHUNKS = 20
-LAG = 3
+CHUNKS = 40
+LAG = 8
 
 
 def gelu_value(values):
@@ -38,10 +38,11 @@
 
 def kernel(
     sizes, cap,
-    merged, cot, text, w, pre, row_out, tok_out, row_in, tok_in,
-    emb, grad,
+    cot_hbm, text_hbm, w_hbm, pre_hbm, bias, row_slot, tok_slot,
+    emb_hbm, grad_hbm,
+    cot, text, w, pre, merged, emb, grad, load_sem, store_sem,
     out_buf, z_buf, relay, x_buf, y_buf, w_far, rows_full, rows_far, flow_in, flow_out, acc,
-    z_send, z_recv, x_send, x_recv, y_send, y_recv,
+    z_send, z_recv, part_send, part_recv, tail_send, tail_recv, x_send, x_recv, y_send, y_recv,
     w_send, w_recv, g_send, g_recv,
     flow_send, flow_recv, fin_send, fin_recv, mate_send, mate_recv,
 ):
@@ -57,7 +58,7 @@
     slots = blocks * 2 * cap
     tokens, width = cot.shape
     half_width = width // 2
-    rows = merged.shape[0]
+    rows, depth = pre.shape
     half_rows = rows // 2
     count, piece = flow_out.shape[0], flow_out.shape[2]
     shape6 = (nz, nx, ny, 2 * cap, half_width)
@@ -81,27 +82,50 @@
     def _():
         pl.semaphore_signal(barrier, inc=1, device_id=up, device_id_type=MESH)
 
-    pl.semaphore_wait(
-        barrier,
-        len(greeted) + (line > 0).astype(jnp.int32) + (line < nl - 1).astype(jnp.int32),
-    )
+    loads = [
+        pltpu.make_async_copy(src, dst, load_sem.at[n])
+        for n, (src, dst) in enumerate(
+            ((cot_hbm, cot), (w_hbm, w), (pre_hbm, pre), (text_hbm, text))
+        )
+    ]
+    for load in loads:
+        load.start()
+
+    def bits(n):
+        return n.bit_length() - 1
+
+    def position(values, sign):
+        peer = lax.shift_right_logical(values, bits(cap))
+        dy = (sign * ((peer & (ny - 1)) - yy)) & (ny - 1)
+        dz = (sign * ((lax.shift_right_logical(peer, bits(ny)) & (nz - 1)) - zh)) & (nz - 1)
+        dx = (sign * (lax.shift_right_logical(peer, bits(ny * nz)) - xx)) & (nx - 1)
+        base = ((dz * nx + dx) * ny + dy) * (2 * cap) + (values & (cap - 1))
+        return jnp.where(values >= 0, base, -1000000)
+
+    def upright(values):
+        wide = jnp.broadcast_to(values, (128, values.shape[1]))
+        return jnp.transpose(wide)[:, :1]
 
     def place(b, source, where):
         total = jnp.zeros((slots, half_width), jnp.float32)
         ids = lax.broadcasted_iota(jnp.int32, (slots, source.shape[0]), 0)
         for h in range(2):
-            hot = (ids == where[...] + h * cap).astype(jnp.bfloat16)
+            hot = (ids == where + h * cap).astype(jnp.bfloat16)
             part = source[:, h * half_width : (h + 1) * half_width]
             total += jnp.dot(hot, part, preferred_element_type=jnp.float32)
         out_buf[b] = total.astype(jnp.bfloat16).reshape(shape6)
 
     def pick(b, where, h):
         ids = lax.broadcasted_iota(jnp.int32, (where.shape[0], slots), 1)
-        hot = (ids == where[...] + h * cap).astype(jnp.bfloat16)
+        hot = (ids == where + h * cap).astype(jnp.bfloat16)
         data = y_buf[b].reshape(slots, half_width)
         return jnp.dot(hot, data, preferred_element_type=jnp.float32)
 
+    wait_peers = (
+        len(greeted) + (line > 0).astype(jnp.int32) + (line < nl - 1).astype(jnp.int32)
+    )
     cut = nx // 2
+    parts, tails = nx * ny, cut * ny
 
     def z_copy(b, n):
         src, dst, peer = (
@@ -127,20 +151,42 @@
             return pltpu.make_async_copy(src, dst, y_recv.at[b, d, 0])
         return remote(src, dst, y_send.at[b, d, f], y_recv.at[b, d, f], y_peer[f])
 
-    def z_start(b):
+    def part_copy(q, side):
+        e, f = q // ny, q % ny
+        src, dst = (out_buf.at[1, 1 + 2 * side, e, f], z_buf.at[1, 2 * side, e, f])
+        return remote(
+            src, dst, part_send.at[side, q], part_recv.at[side, q], (right, left)[side]
+        )
+
+    def tail_copy(q, side):
+        e, f = q // ny, q % ny
+        src, dst = relay.at[1, side, e, f], z_buf.at[1, 1, side * cut + e, f]
+        return remote(
+            src, dst, tail_send.at[side, q], tail_recv.at[side, q], (right, left)[side]
+        )
+
+    def each(count, act):
+        def body(q, carry):
+            for side in range(2):
+                act(q, side)
+            return carry
+
+        lax.fori_loop(0, count, body, 0)
+
+    def z_start(names):
         if nz > 1:
-            for n in range(4):
+            for b, n in names:
                 z_copy(b, n).start()
 
-    def z_forward(b):
+    def z_forward():
         if nz > 1:
             for n in (0, 1):
-                z_copy(b, n).wait_recv()
-                z_copy(b, n + 4).start()
-
-    def z_arrive(b, d):
-        for n in {0: (), 1: (2,), 2: (4, 5), 3: (3,)}[d]:
-            z_copy(b, n).wait_recv()
+                z_copy(0, n).wait_recv()
+                z_copy(0, n + 4).start()
+
+    def z_arrive(d):
+        for n in {1: (2,), 2: (4, 5), 3: (3,)}[d]:
+            z_copy(0, n).wait_recv()
 
     def x_start(b, d):
         for e in list(range(1, nx)) + [0]:
@@ -159,22 +205,46 @@
             y_copy(b, d, f).wait_recv()
 
     w_copy = remote(w, w_far, w_send, w_recv, mate)
+    tok_out = position(tok_slot[...], 1)
+    loads[0].wait()
+    place(0, cot, tok_out)
+    pl.semaphore_wait(barrier, wait_peers)
+    z_start([(0, n) for n in range(4)])
+    x_start(0, 0)
+    loads[1].wait()
     w_copy.start()
-
-    place(0, cot, tok_out)
-    z_start(0)
-    x_start(0, 0)
-    place(1, merged, row_out)
+    loads[2].wait()
+    merged[...] = jnp.zeros_like(merged)
+    deep = 4 * piece
+
+    def forward(i, carry):
+        cols = pl.ds(pl.multiple_of(i * deep, deep), deep)
+        hidden = gelu_value(pre[:, cols].astype(jnp.float32)).astype(jnp.bfloat16)
+        merged[...] += jnp.dot(hidden, w[cols, :], preferred_element_type=jnp.float32)
+        return carry
+
+    lax.fori_loop(0, depth // deep, forward, 0)
+    place(
+        1,
+        (merged[...] + bias[...].astype(jnp.float32)).astype(jnp.bfloat16),
+        position(row_slot[...], 1),
+    )
     y_start(0, 0)
-    z_forward(0)
-    z_start(1)
+    z_forward()
+    z_start([(1, 0), (1, 1)])
     x_start(1, 0)
+    row_in = upright(position(row_slot[...], -1))
+    tok_in = upright(position(tok_slot[...], -1))
     y_start(1, 0)
-    far = [1, 3, 2] if nz > 1 else []
-    for d in far:
-        z_arrive(0, d)
-        x_start(0, d)
-        y_start(0, d)
+    if nz > 1:
+        for d in (1, 3):
+            z_arrive(d)
+            x_start(0, d)
+        for d in (1, 3):
+            y_start(0, d)
+        z_arrive(2)
+        x_start(0, 2)
+        y_start(0, 2)
     for d in range(nz):
         y_arrive(0, d)
 
@@ -186,7 +256,6 @@
     other = pl.ds(pl.multiple_of((1 - core) * half_rows, half_rows), half_rows)
     g_copy = remote(rows_full.at[other], rows_far, g_send, g_recv, mate)
     g_copy.start()
-    z_forward(1)
     w_copy.wait_recv()
     g_copy.wait_recv()
 
@@ -225,7 +294,26 @@
     lag = 1 + LAG * away
     steps = count + 1 + LAG * (nl // 2 + (1 if nl > 1 else 0))
 
+    def dispatch(i):
+        @pl.when(i < parts)
+        def _():
+            for side in range(2):
+                part_copy(i, side).start()
+
+        @pl.when(i == parts)
+        def _():
+            for n in (0, 1):
+                z_copy(1, n).wait_recv()
+
+        @pl.when(jnp.logical_and(i >= parts, i < parts + tails))
+        def _():
+            for side in range(2):
+                tail_copy(i - parts, side).start()
+
     def step(i, carry):
+        if nz > 1:
+            dispatch(i)
+
         @pl.when(i < count)
         def _():
             acc[...] = nt_dot(rows_full[mine, :], w[columns(i), :]) + nt_dot(
@@ -269,23 +357,35 @@
 
         return carry
 
-    first, second = count // 2, count // 2 + 3
-    lax.fori_loop(0, first, step, 0)
-    for d in far:
-        z_arrive(1, d)
-        x_start(1, d)
-    lax.fori_loop(first, second, step, 0)
-    for d in far:
-        y_start(1, d)
-    lax.fori_loop(second, steps, step, 0)
-
+    first = parts + tails + 6
+    marks = (0, first, first + 5, first + 9, steps)
+    lax.fori_loop(marks[0], marks[1], step, 0)
+    if nz > 1:
+        each(parts, lambda q, side: part_copy(q, side).wait_recv())
+        for d in (1, 3):
+            x_start(1, d)
+    lax.fori_loop(marks[1], marks[2], step, 0)
+    if nz > 1:
+        for d in (1, 3):
+            y_start(1, d)
+        each(tails, lambda q, side: tail_copy(q, side).wait_recv())
+        x_start(1, 2)
+    lax.fori_loop(marks[2], marks[3], step, 0)
+    if nz > 1:
+        y_start(1, 2)
+    lax.fori_loop(marks[3], steps, step, 0)
+
+    loads[3].wait()
     for d in range(nz):
         y_arrive(1, d)
     for h in range(2):
         part = pl.ds(h * half_width, half_width)
         emb[:, part] = jnp.where(
-            tok_in[...] >= 0, pick(1, tok_in, h).astype(jnp.bfloat16), text[:, part]
+            tok_in >= 0, pick(1, tok_in, h).astype(jnp.bfloat16), text[:, part]
         )
+
+    emb_store = pltpu.make_async_copy(emb, emb_hbm, store_sem.at[0])
+    emb_store.start()
 
     def drain(i, carry):
         @pl.when(line < middle)
@@ -308,49 +408,53 @@
         mate_block(i).wait_recv()
         return carry
 
-    lax.fori_loop(0, count, drain, 0)
+    groups = 4
+    span = count // groups
+    stores = []
+    for n in range(groups):
+        lax.fori_loop(n * span, (n + 1) * span, drain, 0)
+        cols = pl.ds(n * span * piece, span * piece)
+        store = pltpu.make_async_copy(grad.at[:, cols], grad_hbm.at[:, cols], store_sem.at[n + 1])
+        store.start()
+        stores.append(store)
     w_copy.wait_send()
     g_copy.wait_send()
+    if nz > 1:
+        for n in range(6):
+            z_copy(0, n).wait_send()
+        for n in range(2):
+            z_copy(1, n).wait_send()
+        each(parts, lambda q, side: part_copy(q, side).wait_send())
+        each(tails, lambda q, side: tail_copy(q, side).wait_send())
     for b in range(2):
-        if nz > 1:
-            for n in range(6):
-                z_copy(b, n).wait_send()
         for d in range(nz):
             for e in range(1, nx):
                 x_copy(b, d, e).wait_send()
             for f in range(1, ny):
                 y_copy(b, d, f).wait_send()
+    emb_store.wait()
+    for store in stores:
+        store.wait()
 
 
 def shards(cap, pre_act, w_out, b_out, row_slot, ctx_slot, text_rows, cotangent):
     nx, nz, ny, nl = (lax.axis_size(a) for a in ("x", "zh", "y", "zl"))
-    xx, zh, yy = (lax.axis_index(a) for a in ("x", "zh", "y"))
     rows, depth = pre_act.shape
     tokens, width = cotangent.shape
-    hidden = gelu_value(pre_act.astype(jnp.float32)).astype(jnp.bfloat16)
-    merged = (
-        jnp.dot(hidden, w_out, preferred_element_type=jnp.float32) + b_out.astype(jnp.float32)
-    ).astype(jnp.bfloat16)
-
-    def position(values, sign):
-        peer, slot = values // cap, values % cap
-        dx = (sign * (peer // (nz * ny) - xx)) % nx
-        dz = (sign * ((peer // ny) % nz - zh)) % nz
-        dy = (sign * (peer % ny - yy)) % ny
-        base = ((dz * nx + dx) * ny + dy) * 2 * cap + slot
-        return jnp.where(values >= 0, base, -1000000)
-
-    row_out = position(row_slot, 1).reshape(1, rows)
-    tok_out = position(ctx_slot, 1).reshape(1, tokens)
-    row_in = position(row_slot, -1).reshape(rows, 1)
-    tok_in = position(ctx_slot, -1).reshape(tokens, 1)
-
     half_width, half_rows = width // 2, rows // 2
     piece = depth // CHUNKS
     block = (nx, ny, 2 * cap, half_width)
     dma = pltpu.SemaphoreType.DMA
     bf16 = jnp.bfloat16
     scratch = [
+        pltpu.VMEM((tokens, width), bf16),
+        pltpu.VMEM((tokens, width), bf16),
+        pltpu.VMEM((depth, width), bf16),
+        pltpu.VMEM((rows, depth), bf16),
+        pltpu.VMEM((rows, width), jnp.float32),
+        pltpu.VMEM((tokens, width), bf16),
+        pltpu.VMEM((rows, depth), bf16),
+        dma((4,)), dma((5,)),
         pltpu.VMEM((2, nz, *block), bf16),
         pltpu.VMEM((2, max(nz - 1, 1), *block), bf16),
         pltpu.VMEM((2, 2, max(nx // 2, 1), *block[1:]), bf16),
@@ -363,6 +467,8 @@
         pltpu.VMEM((CHUNKS, half_rows, piece), bf16),
         pltpu.VMEM((half_rows, piece), jnp.float32),
         dma((2, 6)), dma((2, 6)),
+        dma((2, nx * ny)), dma((2, nx * ny)),
+        dma((2, max(nx // 2 * ny, 1))), dma((2, max(nx // 2 * ny, 1))),
         dma((2, nz, nx)), dma((2, nz, nx)),
         dma((2, nz, ny)), dma((2, nz, ny)),
         dma, dma, dma, dma,
@@ -376,13 +482,17 @@
             jax.ShapeDtypeStruct((tokens, width), bf16),
             jax.ShapeDtypeStruct((rows, depth), bf16),
         ),
-        in_specs=[pl.BlockSpec(memory_space=pltpu.VMEM)] * 9,
-        out_specs=(pl.BlockSpec(memory_space=pltpu.VMEM),) * 2,
+        in_specs=[pl.BlockSpec(memory_space=pl.ANY)] * 4
+        + [pl.BlockSpec(memory_space=pltpu.VMEM)] * 3,
+        out_specs=(pl.BlockSpec(memory_space=pl.ANY),) * 2,
         scratch_shapes=scratch,
         compiler_params=pltpu.CompilerParams(
             collective_id=0, has_side_effects=True, vmem_limit_bytes=60 << 20
         ),
-    )(merged, cotangent, text_rows, w_out, pre_act, row_out, tok_out, row_in, tok_in)
+    )(
+        cotangent, text_rows, w_out, pre_act,
+        b_out.reshape(1, width), row_slot.reshape(1, rows), ctx_slot.reshape(1, tokens),
+    )
 
 
 def build(mesh, nx, nz, nl, cap):

time: 207 us -> 197 us (0.952)
  matrix products: 5.52 us -> 0 us
  other arithmetic: 4.68 us -> 0 us
    dot_general x1 -> x0, matrix products: 5.52 us -> none  [shards(): jnp.dot(hidden, w_out, preferred_element_type=jnp.float32)]
    select_n x4 -> x0, other arithmetic: 4 us -> none  [position(): return jnp.where(values >= 0, base, -1000000)]
where the time goes in v2:
time: 197 us
  Pallas kernels  190 us (96%)
  local copies, waits for them, and re-layouts  6.53 us (3%)
    pallas_call x1, Pallas kernels, shards(): pl.pallas_call(functools.partial(kernel, (nz, nx, ny, nl), cap), out_shap...  190 us
    unnamed x2, local copies, waits for them, and re-layouts  5.27 us

profile of v2, /device:TPU:1, one launch (start us, length us, event | category | flops | bytes accessed | tf_op | source)
XLA Modules:
  0.0 197.0 jit_solution(16675699168537621741)
XLA Ops:
  0.6 1.3 reshape.13.bias
  1.9 189.8 %shard_map.86 = (bf16[512,512]{1,0:T(8,128)(2,1)}, bf16[256,5120]{1,0:T(8,128)(2,1)}) custom-call(bf16[512,512]{1,0:T(8,128)(2,1)} %cot_hbm.1, bf16[512,512]{1,0:T(8,128)(2,1)} %text_hbm.1, bf16[5120,512]{1,0:T(8,128)(2,1)} %w_hbm.1, bf16[256,5120]{1,0:T(8,128)(2,1)} %pre_hbm.1, bf16[1,512]{1,0:T(2,128)(2,1)} %reshape.13.bias, s32[1,256]{1,0:T(1,128)} %bitcast.3, ...), custom_call_target="tpu_custom_call" | custom-call | tf_op jit(solution)/shard_map/pallas_call | solution.py:479
  191.7 1.9 copy.11
  193.6 3.4 %copy.12 = bf16[256,5120]{1,0:T(8,128)(2,1)} copy(bf16[256,5120]{1,0:T(8,128)(2,1)} %get-tuple-element.5) | data formatting | bytes 5242880

commit v3 on v2

--- a/solution.py
+++ b/solution.py
@@ -11,6 +11,7 @@
 MESH = pl.DeviceIdType.MESH
 CHUNKS = 40
 LAG = 8
+EARLY = 10
 
 
 def gelu_value(values):
@@ -42,7 +43,7 @@
     emb_hbm, grad_hbm,
     cot, text, w, pre, merged, emb, grad, load_sem, store_sem,
     out_buf, z_buf, relay, x_buf, y_buf, w_far, rows_full, rows_far, flow_in, flow_out, acc,
-    z_send, z_recv, part_send, part_recv, tail_send, tail_recv, x_send, x_recv, y_send, y_recv,
+    z_send, z_recv, x_send, x_recv, y_send, y_recv,
     w_send, w_recv, g_send, g_recv,
     flow_send, flow_recv, fin_send, fin_recv, mate_send, mate_recv,
 ):
@@ -125,7 +126,6 @@
         len(greeted) + (line > 0).astype(jnp.int32) + (line < nl - 1).astype(jnp.int32)
     )
     cut = nx // 2
-    parts, tails = nx * ny, cut * ny
 
     def z_copy(b, n):
         src, dst, peer = (
@@ -151,28 +151,6 @@
             return pltpu.make_async_copy(src, dst, y_recv.at[b, d, 0])
         return remote(src, dst, y_send.at[b, d, f], y_recv.at[b, d, f], y_peer[f])
 
-    def part_copy(q, side):
-        e, f = q // ny, q % ny
-        src, dst = (out_buf.at[1, 1 + 2 * side, e, f], z_buf.at[1, 2 * side, e, f])
-        return remote(
-            src, dst, part_send.at[side, q], part_recv.at[side, q], (right, left)[side]
-        )
-
-    def tail_copy(q, side):
-        e, f = q // ny, q % ny
-        src, dst = relay.at[1, side, e, f], z_buf.at[1, 1, side * cut + e, f]
-        return remote(
-            src, dst, tail_send.at[side, q], tail_recv.at[side, q], (right, left)[side]
-        )
-
-    def each(count, act):
-        def body(q, carry):
-            for side in range(2):
-                act(q, side)
-            return carry
-
-        lax.fori_loop(0, count, body, 0)
-
     def z_start(names):
         if nz > 1:
             for b, n in names:
@@ -184,9 +162,9 @@
                 z_copy(0, n).wait_recv()
                 z_copy(0, n + 4).start()
 
-    def z_arrive(d):
+    def z_arrive(b, d):
         for n in {1: (2,), 2: (4, 5), 3: (3,)}[d]:
-            z_copy(0, n).wait_recv()
+            z_copy(b, n).wait_recv()
 
     def x_start(b, d):
         for e in list(range(1, nx)) + [0]:
@@ -232,17 +210,50 @@
     y_start(0, 0)
     z_forward()
     z_start([(1, 0), (1, 1)])
+    low = line <= middle
+    high = line > middle
+
+    def outward(right_copy, left_copy, relays):
+        def go(n, relayed):
+            if relays:
+                z_copy(1, relayed).wait_recv()
+            z_copy(1, n).start()
+
+        @pl.when(low)
+        def _():
+            go(left_copy, 1)
+
+        @pl.when(high)
+        def _():
+            go(right_copy, 0)
+
+    def inward(right_copy, left_copy, relays):
+        def go(n, relayed):
+            if relays:
+                z_copy(1, relayed).wait_recv()
+            z_copy(1, n).start()
+
+        @pl.when(low)
+        def _():
+            go(right_copy, 0)
+
+        @pl.when(high)
+        def _():
+            go(left_copy, 1)
+
+    if nz > 1:
+        outward(2, 3, False)
     x_start(1, 0)
     row_in = upright(position(row_slot[...], -1))
     tok_in = upright(position(tok_slot[...], -1))
     y_start(1, 0)
     if nz > 1:
         for d in (1, 3):
-            z_arrive(d)
+            z_arrive(0, d)
             x_start(0, d)
         for d in (1, 3):
             y_start(0, d)
-        z_arrive(2)
+        z_arrive(0, 2)
         x_start(0, 2)
         y_start(0, 2)
     for d in range(nz):
@@ -295,20 +306,14 @@
     steps = count + 1 + LAG * (nl // 2 + (1 if nl > 1 else 0))
 
     def dispatch(i):
-        @pl.when(i < parts)
-        def _():
-            for side in range(2):
-                part_copy(i, side).start()
-
-        @pl.when(i == parts)
-        def _():
-            for n in (0, 1):
-                z_copy(1, n).wait_recv()
-
-        @pl.when(jnp.logical_and(i >= parts, i < parts + tails))
-        def _():
-            for side in range(2):
-                tail_copy(i - parts, side).start()
+        @pl.when(i == EARLY)
+        def _():
+            outward(4, 5, True)
+
+        @pl.when(i == count)
+        def _():
+            inward(2, 3, False)
+            inward(4, 5, True)
 
     def step(i, carry):
         if nz > 1:
@@ -357,23 +362,16 @@
 
         return carry
 
-    first = parts + tails + 6
-    marks = (0, first, first + 5, first + 9, steps)
-    lax.fori_loop(marks[0], marks[1], step, 0)
-    if nz > 1:
-        each(parts, lambda q, side: part_copy(q, side).wait_recv())
-        for d in (1, 3):
-            x_start(1, d)
-    lax.fori_loop(marks[1], marks[2], step, 0)
+    lax.fori_loop(0, steps, step, 0)
     if nz > 1:
         for d in (1, 3):
+            z_arrive(1, d)
+            x_start(1, d)
+        for d in (1, 3):
             y_start(1, d)
-        each(tails, lambda q, side: tail_copy(q, side).wait_recv())
+        z_arrive(1, 2)
         x_start(1, 2)
-    lax.fori_loop(marks[2], marks[3], step, 0)
-    if nz > 1:
         y_start(1, 2)
-    lax.fori_loop(marks[3], steps, step, 0)
 
     loads[3].wait()
     for d in range(nz):
@@ -420,12 +418,9 @@
     w_copy.wait_send()
     g_copy.wait_send()
     if nz > 1:
-        for n in range(6):
-            z_copy(0, n).wait_send()
-        for n in range(2):
-            z_copy(1, n).wait_send()
-        each(parts, lambda q, side: part_copy(q, side).wait_send())
-        each(tails, lambda q, side: tail_copy(q, side).wait_send())
+        for b in range(2):
+            for n in range(6):
+                z_copy(b, n).wait_send()
     for b in range(2):
         for d in range(nz):
             for e in range(1, nx):
@@ -467,8 +462,6 @@
         pltpu.VMEM((CHUNKS, half_rows, piece), bf16),
         pltpu.VMEM((half_rows, piece), jnp.float32),
         dma((2, 6)), dma((2, 6)),
-        dma((2, nx * ny)), dma((2, nx * ny)),
-        dma((2, max(nx // 2 * ny, 1))), dma((2, max(nx // 2 * ny, 1))),
         dma((2, nz, nx)), dma((2, nz, nx)),
         dma((2, nz, ny)), dma((2, nz, ny)),
         dma, dma, dma, dma,

time: 197 us -> 201 us (1.020)
  Pallas kernels: 190 us -> 193 us
    pallas_call x1, Pallas kernels: 190 us -> 193 us  [shards(): pl.pallas_call(functools.partial(kernel, (nz, nx, ny, nl), cap), out_shap...]
where the time goes in v3:
time: 201 us
  Pallas kernels  193 us (96%)
  local copies, waits for them, and re-layouts  6.53 us (3%)
    pallas_call x1, Pallas kernels, shards(): pl.pallas_call(functools.partial(kernel, (nz, nx, ny, nl), cap), out_shap...  193 us
    unnamed x2, local copies, waits for them, and re-layouts  5.27 us

profile of v3, /device:TPU:1, one launch (start us, length us, event | category | flops | bytes accessed | tf_op | source)
XLA Modules:
  0.0 200.6 jit_solution(17971050994772813594)
XLA Ops:
  0.6 1.3 reshape.13.bias
  1.9 193.4 %shard_map.86 = (bf16[512,512]{1,0:T(8,128)(2,1)}, bf16[256,5120]{1,0:T(8,128)(2,1)}) custom-call(bf16[512,512]{1,0:T(8,128)(2,1)} %cot_hbm.1, bf16[512,512]{1,0:T(8,128)(2,1)} %text_hbm.1, bf16[5120,512]{1,0:T(8,128)(2,1)} %w_hbm.1, bf16[256,5120]{1,0:T(8,128)(2,1)} %pre_hbm.1, bf16[1,512]{1,0:T(2,128)(2,1)} %reshape.13.bias, s32[1,256]{1,0:T(1,128)} %bitcast.3, ...), custom_call_target="tpu_custom_call" | custom-call | tf_op jit(solution)/shard_map/pallas_call | solution.py:472
  195.3 1.9 copy.11
  197.2 3.4 %copy.12 = bf16[256,5120]{1,0:T(8,128)(2,1)} copy(bf16[256,5120]{1,0:T(8,128)(2,1)} %get-tuple-element.5) | data formatting | bytes 5242880

commit v4 on v3

--- a/solution.py
+++ b/solution.py
@@ -11,7 +11,6 @@
 MESH = pl.DeviceIdType.MESH
 CHUNKS = 40
 LAG = 8
-EARLY = 10
 
 
 def gelu_value(values):
@@ -156,11 +155,11 @@
             for b, n in names:
                 z_copy(b, n).start()
 
-    def z_forward():
+    def z_forward(b):
         if nz > 1:
             for n in (0, 1):
-                z_copy(0, n).wait_recv()
-                z_copy(0, n + 4).start()
+                z_copy(b, n).wait_recv()
+                z_copy(b, n + 4).start()
 
     def z_arrive(b, d):
         for n in {1: (2,), 2: (4, 5), 3: (3,)}[d]:
@@ -208,41 +207,9 @@
         position(row_slot[...], 1),
     )
     y_start(0, 0)
-    z_forward()
+    z_forward(0)
     z_start([(1, 0), (1, 1)])
-    low = line <= middle
-    high = line > middle
-
-    def outward(right_copy, left_copy, relays):
-        def go(n, relayed):
-            if relays:
-                z_copy(1, relayed).wait_recv()
-            z_copy(1, n).start()
-
-        @pl.when(low)
-        def _():
-            go(left_copy, 1)
-
-        @pl.when(high)
-        def _():
-            go(right_copy, 0)
-
-    def inward(right_copy, left_copy, relays):
-        def go(n, relayed):
-            if relays:
-                z_copy(1, relayed).wait_recv()
-            z_copy(1, n).start()
-
-        @pl.when(low)
-        def _():
-            go(right_copy, 0)
-
-        @pl.when(high)
-        def _():
-            go(left_copy, 1)
-
-    if nz > 1:
-        outward(2, 3, False)
+    z_start([(1, 2), (1, 3)])
     x_start(1, 0)
     row_in = upright(position(row_slot[...], -1))
     tok_in = upright(position(tok_slot[...], -1))
@@ -267,6 +234,7 @@
     other = pl.ds(pl.multiple_of((1 - core) * half_rows, half_rows), half_rows)
     g_copy = remote(rows_full.at[other], rows_far, g_send, g_recv, mate)
     g_copy.start()
+    z_forward(1)
     w_copy.wait_recv()
     g_copy.wait_recv()
 
@@ -305,20 +273,7 @@
     lag = 1 + LAG * away
     steps = count + 1 + LAG * (nl // 2 + (1 if nl > 1 else 0))
 
-    def dispatch(i):
-        @pl.when(i == EARLY)
-        def _():
-            outward(4, 5, True)
-
-        @pl.when(i == count)
-        def _():
-            inward(2, 3, False)
-            inward(4, 5, True)
-
     def step(i, carry):
-        if nz > 1:
-            dispatch(i)
-
         @pl.when(i < count)
         def _():
             acc[...] = nt_dot(rows_full[mine, :], w[columns(i), :]) + nt_dot(
@@ -362,16 +317,17 @@
 
         return carry
 
-    lax.fori_loop(0, steps, step, 0)
+    first, second = count // 2, count // 2 + 6
+    lax.fori_loop(0, first, step, 0)
     if nz > 1:
-        for d in (1, 3):
+        for d in (1, 3, 2):
             z_arrive(1, d)
             x_start(1, d)
-        for d in (1, 3):
+    lax.fori_loop(first, second, step, 0)
+    if nz > 1:
+        for d in (1, 3, 2):
             y_start(1, d)
-        z_arrive(1, 2)
-        x_start(1, 2)
-        y_start(1, 2)
+    lax.fori_loop(second, steps, step, 0)
 
     loads[3].wait()
     for d in range(nz):

time: 201 us -> 183 us (0.910)
  Pallas kernels: 193 us -> 176 us
    pallas_call x1, Pallas kernels: 193 us -> 176 us  [shards(): pl.pallas_call(functools.partial(kernel, (nz, nx, ny, nl), cap), out_shap...]
where the time goes in v4:
time: 183 us
  Pallas kernels  176 us (96%)
  local copies, waits for them, and re-layouts  6.53 us (4%)
    pallas_call x1, Pallas kernels, shards(): pl.pallas_call(functools.partial(kernel, (nz, nx, ny, nl), cap), out_shap...  176 us
    unnamed x2, local copies, waits for them, and re-layouts  5.27 us

profile of v4, /device:TPU:1, one launch (start us, length us, event | category | flops | bytes accessed | tf_op | source)
XLA Modules:
  0.0 183.0 jit_solution(5435397354604554571)
XLA Ops:
  0.6 1.3 reshape.13.bias
  1.9 175.9 %shard_map.86 = (bf16[512,512]{1,0:T(8,128)(2,1)}, bf16[256,5120]{1,0:T(8,128)(2,1)}) custom-call(bf16[512,512]{1,0:T(8,128)(2,1)} %cot_hbm.1, bf16[512,512]{1,0:T(8,128)(2,1)} %text_hbm.1, bf16[5120,512]{1,0:T(8,128)(2,1)} %w_hbm.1, bf16[256,5120]{1,0:T(8,128)(2,1)} %pre_hbm.1, bf16[1,512]{1,0:T(2,128)(2,1)} %reshape.13.bias, s32[1,256]{1,0:T(1,128)} %bitcast.3, ...), custom_call_target="tpu_custom_call" | custom-call | tf_op jit(solution)/shard_map/pallas_call | solution.py:428
  177.8 1.9 %copy.11 = bf16[512,512]{1,0:T(8,128)(2,1)} copy(bf16[512,512]{1,0:T(8,128)(2,1)} %get-tuple-element.4) | data formatting | bytes 1048576
  179.6 3.4 %copy.12 = bf16[256,5120]{1,0:T(8,128)(2,1)} copy(bf16[256,5120]{1,0:T(8,128)(2,1)} %get-tuple-element.5) | data formatting | bytes 5242880
